TPU v7x, 32 devices: a whole 2x2x4 slice. The times are simulated.
32 devices in a mesh: section: 2 (over y), expert: 16 (over z, x, core).
Axes of the slice: x: 2, y: 2, z: 4, core: 2. Of those that a mesh axis runs over, the one named last changes fastest.
Arguments:
- tokens: bfloat16 [2048, 7168], P('expert', 'section'), may hold values from -6 to 6
- exponents: int32 [2048, 56], P('expert', 'section'), may hold values from -9 to -5
- expert_ids: int32 [2048, 8], P('expert'), may hold values from 0 to 15, all different within a row; in each aligned block of 128 rows (0 to 127, 128 to 255, ...) at most 80 rows name the same one
- affinity: float32 [2048, 8], P('expert'), may hold values from 0.1 to 1
- w_gate: bfloat16 [16, 7168, 2048], P('expert', None, 'section'), may hold values from -0.0625 to 0.0625
- w_up: bfloat16 [16, 7168, 2048], P('expert', None, 'section'), may hold values from -0.0625 to 0.0625
- w_down: bfloat16 [16, 2048, 7168], P('expert', 'section'), may hold values from -0.125 to 0.125
Outputs:
- moe_out: bfloat16 [2048, 7168], P('expert', 'section')
Inputs may be any that keep to these rules, and one draw needn't show every extreme that they name: `expert_ids`: each row names 8 different experts. In the 128 rows of one token group no expert is named more than 80 times, a bound that some block reaches.
All inputs are finite; a program needn't handle non-finite values.
Results may differ from a plain program's by a relative error of at most 0.012.
Values may be sent and summed in bfloat16 or wider, within the bound.
No kernel may reach another device: no remote copies, remote signals or barrier semaphores. Data moves between devices by JAX's collectives and lax.ppermute only.
A program may use at most 192 MiB of HBM per device.

v0:
```python
import jax
import jax.numpy as jnp
from jax import lax
from jax.sharding import PartitionSpec as P

quant_limit = 448.0
route_scaling = 2.5


def slot_positions(ids, capacity, experts):
    flat = ids.reshape(-1)
    marks = (flat[:, None] == jnp.arange(experts, dtype=jnp.int32)[None, :]).astype(jnp.int32)
    before = jnp.cumsum(marks, axis=0) - marks
    slot = jnp.sum(before * marks, axis=1)
    return (flat * capacity + slot).reshape(ids.shape)


def body(tokens, exponents, expert_ids, affinity, w_gate, w_up, w_down):
    tok_rows, width = tokens.shape
    tile_count = width // 128
    top_count = expert_ids.shape[1]
    section_count = lax.axis_size("section")
    expert_count = lax.axis_size("expert")
    capacity = min(tok_rows, tok_rows * top_count * 5 // (4 * expert_count))
    slot_total = expert_count * capacity
    scales = jnp.exp2(exponents.astype(jnp.float32))
    tiles = tokens.astype(jnp.float32).reshape(tok_rows, tile_count, 128) / scales[:, :, None]
    quant = jnp.clip(tiles, -quant_limit, quant_limit).astype(jnp.bfloat16).reshape(tok_rows, width)
    slot_index = slot_positions(expert_ids, capacity, expert_count)
    columns = jnp.arange(slot_total, dtype=jnp.int32)
    select = jnp.any(slot_index[:, :, None] == columns[None, None, :], axis=1)
    contract = (((0,), (0,)), ((), ()))
    send_tiles = lax.dot_general(
        select.astype(jnp.bfloat16), quant, contract, preferred_element_type=jnp.float32
    ).astype(jnp.bfloat16)
    send_scales = lax.dot_general(
        select.astype(jnp.float32), scales, contract, precision=lax.Precision.HIGHEST
    ).astype(jnp.bfloat16)
    got_tiles, got_scales = (
        lax.all_to_all(
            send_tiles.reshape(expert_count, capacity, width),
            "expert",
            split_axis=0,
            concat_axis=0,
            tiled=True,
        ),
        lax.all_to_all(
            send_scales.reshape(expert_count, capacity, tile_count),
            "expert",
            split_axis=0,
            concat_axis=0,
            tiled=True,
        ),
    )
    all_tiles, all_scales = (
        lax.all_gather(got_tiles[None], "section", axis=0, tiled=True),
        lax.all_gather(got_scales[None], "section", axis=0, tiled=True),
    )
    restored = (
        all_tiles.reshape(section_count, expert_count, capacity, tile_count, 128)
        * all_scales[..., None]
    ).reshape(section_count, slot_total, width)
    hidden_local = w_gate.shape[2]
    gate = jnp.einsum(
        "srd,sdf->rf",
        restored,
        w_gate[0].reshape(section_count, width, hidden_local),
        preferred_element_type=jnp.float32,
    )
    up = jnp.einsum(
        "srd,sdf->rf",
        restored,
        w_up[0].reshape(section_count, width, hidden_local),
        preferred_element_type=jnp.float32,
    )
    hidden = (jax.nn.silu(gate) * up).astype(jnp.bfloat16)
    partial_rows = jnp.einsum(
        "rf,fsd->srd",
        hidden,
        w_down[0].reshape(hidden_local, section_count, width),
        preferred_element_type=jnp.float32,
    ).astype(jnp.bfloat16)
    summed = lax.psum_scatter(partial_rows, "section", scatter_dimension=0, tiled=True).astype(
        jnp.float32
    )
    summed_rows = summed.astype(jnp.bfloat16).reshape(expert_count, capacity, width)
    expert_rows = lax.all_to_all(summed_rows, "expert", split_axis=0, concat_axis=0, tiled=True)
    flat_rows = expert_rows.reshape(slot_total, width)
    picked = jnp.take(flat_rows, slot_index, axis=0)
    route_weight = route_scaling * affinity / jnp.sum(affinity, axis=1, keepdims=True)
    total = jnp.sum(picked.astype(jnp.float32) * route_weight[:, :, None], axis=1)
    return total.astype(jnp.bfloat16)


def solution(mesh):
    return jax.shard_map(
        body,
        mesh=mesh,
        in_specs=(
            P("expert", "section"),
            P("expert", "section"),
            P("expert", None),
            P("expert", None),
            P("expert", None, "section"),
            P("expert", None, "section"),
            P("expert", "section", None),
        ),
        out_specs=P("expert", "section"),
        check_vma=False,
    )
```

profile of v0, /device:TPU:11, one launch (start us, length us, event | category | flops | bytes accessed | tf_op | source)
XLA Modules:
  0.0 986.0 jit_solution(10012667298380749259)
XLA Ops:
  6.5 0.0 all-gather.4.cloned.1.call-start
  6.5 0.8 copy.61
  7.3 0.1 eq.42
  7.4 0.1 eq.38
  7.5 4.5 reduce-window.6
  12.0 0.1 slice.10
  12.1 0.1 copy.63
  12.3 0.1 copy.64
  12.4 0.1 broadcast_add_fusion
  12.5 0.1 reduce_sum.30
  12.6 1.3 compare_and_fusion
  13.9 0.0 copy-start
  13.9 0.1 copy.67
  14.0 0.5 copy-done
  14.5 1.6 fusion.6
  16.2 1.6 copy.68
  17.7 0.7 multiply_exponential_fusion
  18.4 0.2 fusion.9
  18.7 2.6 convolution_convert_fusion.1
  21.3 205.4 %all_to_all.15 = bf16[16,80,3584]{2,1,0:T(8,128)(2,1)} all-to-all(bf16[16,80,3584]{2,1,0:T(8,128)(2,1)S(1)} %bitcast.71), channel_id=1, replica_groups=mesh['section'=2,'expert'=16] {'expert'}, dimensions={0} | all-to-all | bytes 18350080 | tf_op jit(solution)/shard_map/all_to_all | solution.py:40
  226.7 0.0 copy-start.3
  226.7 0.0 all-gather.4.cloned.1.call-update
  226.7 0.7 copy-done.3
  227.4 0.3 convolution_convert_fusion.2
  227.7 0.2 reshape.59
  227.9 0.7 copy.69
  228.6 5.7 all-to-all-start.1
  234.2 0.0 reduce-scatter.2.cloned.1.call-start
  234.3 33.0 %reshape_squeeze.11 = bf16[1024,2,3584]{2,1,0:T(2,128)(2,1)} reshape(bf16[1,1024,7168]{2,1,0:T(8,128)(2,1)} %param.13) | data formatting | bytes 29360128 | tf_op jit(solution)/shard_map/reshape;squeeze | solution.py:80
  267.2 0.0 all-to-all-done.1
  267.3 8.5 all-gather.1
  275.8 0.4 copy.71
  276.2 13.6 %mul.47 = bf16[2,16,80,28,128]{4,3,2,1,0:T(8,128)(2,1)} broadcast(bf16[2,16,80,28]{3,2,1,0:T(8,128)(2,1)S(1)} %copy.71), dimensions={0,1,2,3} | broadcast | bytes 18493440 | tf_op jit(solution)/shard_map/mul | solution.py:60
  289.8 29.7 %mul.48 = bf16[2,1280,3584]{2,1,0:T(8,128)(2,1)} reshape(bf16[2,16,80,28,128]{4,3,2,1,0:T(8,128)(2,1)} %mul.47) | data formatting | bytes 36700160 | tf_op jit(solution)/shard_map/mul | solution.py:60
  319.5 128.6 %all-gather.4.cloned.1.call-done = bf16[32,80,3584]{2,1,0:T(8,128)(2,1)} async-done(((bf16[16,80,3584]{2,1,0:T(8,128)(2,1)}), bf16[32,80,3584]{2,1,0:T(8,128)(2,1)}) %all-gather.4.cloned.1.call-update) | async-done | bytes 18350096 | tf_op jit(solution)/shard_map/all_gather | solution.py:56
  448.1 12.9 %bitcast_multiply_fusion = bf16[2,1280,3584]{2,1,0:T(8,128)(2,1)S(1)} fusion(bf16[2,1280,3584]{2,1,0:T(8,128)(2,1)} %mul.48, bf16[2,1280,3584]{2,1,0:T(8,128)(2,1)} %bitcast.72), kind=kLoop, calls=%fused_computation.2 | loop fusion | flops 9175040 | bytes 55050240 | tf_op jit(solution)/shard_map/mul | solution.py:60
  461.0 23.7 %fusion.15 = f32[1280,1024,1]{1,0,2:T(8,128)} fusion(bf16[2,1280,3584]{2,1,0:T(8,128)(2,1)S(1)} %bitcast_multiply_fusion, bf16[2,3584,1024]{2,1,0:T(8,128)(2,1)} %bitcast.77), kind=kOutput, calls=%fused_computation.37 | convolution fusion | flops 18790481920 | bytes 38273024 | tf_op jit(solution)/shard_map/srd,sdf->rf/dot_general | solution.py:70
  484.7 23.6 %fusion.7 = bf16[1280,1024,1]{1,0,2:T(8,128)(2,1)S(1)} fusion(f32[1280,1024,1]{1,0,2:T(8,128)} %fusion.15, bf16[2,1280,3584]{2,1,0:T(8,128)(2,1)S(1)} %bitcast_multiply_fusion, bf16[2,3584,1024]{2,1,0:T(8,128)(2,1)} %bitcast.78), kind=kOutput, calls=%fused_computation.17 | convolution fusion | flops 18798346240 | bytes 40894464 | tf_op jit(solution)/shard_map/srd,sdf->rf/dot_general | solution.py:64
  508.2 26.9 %fusion = bf16[2,1280,3584]{2,1,0:T(8,128)(2,1)} fusion(bf16[1280,1024,1]{1,0,2:T(8,128)(2,1)S(1)} %fusion.7, bf16[1024,2,3584]{2,1,0:T(2,128)(2,1)} %reshape_squeeze.11), kind=kOutput, calls=%fused_computation.3 | convolution fusion | flops 18799656960 | bytes 35651584 | tf_op jit(solution)/shard_map/rf,fsd->srd/dot_general | solution.py:77
  535.1 0.0 reduce-scatter.2.cloned.1.call-update
  535.1 206.3 %reduce-scatter.2.cloned.1.call-done = bf16[1,1280,3584]{2,1,0:T(8,128)(2,1)} async-done(((bf16[2,1280,3584]{2,1,0:T(8,128)(2,1)}), bf16[1,1280,3584]{2,1,0:T(8,128)(2,1)}) %reduce-scatter.2.cloned.1.call-update) | async-done | bytes 9175056 | tf_op jit(solution)/shard_map/reduce_scatter | solution.py:83
  741.4 0.0 copy-start.1
  741.4 0.0 copy-start.4
  741.4 0.0 copy-start.2
  741.4 6.6 all-to-all-start.2
  748.0 0.0 copy-done.1
  748.0 0.1 copy.73
  748.1 0.1 reshape.64
  748.2 0.0 copy-done.4
  748.3 0.1 copy.66
  748.4 0.0 copy-done.2
  748.4 0.1 copy.74
  748.5 198.7 %all-to-all-done.2 = bf16[16,80,3584]{2,1,0:T(8,128)(2,1)} async-done(((bf16[16,80,3584]{2,1,0:T(8,128)(2,1)}), bf16[16,80,3584]{2,1,0:T(8,128)(2,1)}, u32[]{:S(2)}, u32[]{:S(2)}) %all-to-all-start.2) | async-done | bytes 9175072 | tf_op jit(solution)/shard_map/all_to_all | solution.py:87
  947.2 18.6 %gather_fusion = bf16[1024,3584]{1,0:T(8,128)(2,1)} fusion(bf16[1280,3584]{1,0:T(8,128)(2,1)} %bitcast.13, s32[1024]{0:T(1024)S(1)} %broadcast_clamp_fusion), kind=kCustom, calls=%fused_computation | custom fusion | bytes 14684160 | tf_op jit(solution)/shard_map/jit(_take)/gather | solution.py:89
  965.8 13.3 %multiply_reduce_fusion = bf16[128,3584]{1,0:T(8,128)(2,1)} fusion(bf16[1024,3584]{1,0:T(8,128)(2,1)} %gather_fusion, f32[128,8]{1,0:T(8,128)S(1)} %copy.74, pred[128,8]{1,0:T(8,128)(4,1)S(1)} %copy.66), kind=kLoop, calls=%fused_computation.6 | loop fusion | flops 14221312 | bytes 8262656 | tf_op jit(solution)/shard_map/reduce_sum | solution.py:91
  (10 shorter events, 0.2 us)
Async XLA Ops:
  6.5 441.5 %all-gather.4.cloned.1.call-start = ((), (), s32[]{:S(2)}) async-start(), calls=%async_computation.5 | async-start | bytes 27525120 | tf_op jit(solution)/shard_map/all_gather | solution.py:56
  13.9 0.6 copy-start
  226.7 0.7 copy-start.3
  228.6 38.7 %all-to-all-start.1 = ((bf16[16,80,28]{1,2,0:T(8,128)(2,1)}), bf16[16,80,28]{1,2,0:T(8,128)(2,1)S(1)}, u32[]{:S(2)}, u32[]{:S(2)}) async-start(bf16[16,80,28]{1,2,0:T(8,128)(2,1)} %copy.69), calls=%async_computation.1 | async-start | bytes 262144 | tf_op jit(solution)/shard_map/all_to_all | solution.py:47
  234.2 507.2 %reduce-scatter.2.cloned.1.call-start = ((), (), s32[]{:S(2)}) async-start(), calls=%async_computation.4 | async-start | bytes 27525120 | tf_op jit(solution)/shard_map/reduce_scatter | solution.py:83
  741.4 6.6 copy-start.1
  741.4 6.9 copy-start.4
  741.4 7.0 copy-start.2
  741.4 205.8 %all-to-all-start.2 = ((bf16[16,80,3584]{2,1,0:T(8,128)(2,1)}), bf16[16,80,3584]{2,1,0:T(8,128)(2,1)}, u32[]{:S(2)}, u32[]{:S(2)}) async-start(bf16[16,80,3584]{2,1,0:T(8,128)(2,1)} %bitcast.73), calls=%async_computation.3 | async-start | bytes 18350080 | tf_op jit(solution)/shard_map/all_to_all | solution.py:87
Sparse Core Ops, SparseCore 0:
  226.8 221.2 all-gather.3
  535.2 206.0 reduce-scatter.1
where the time goes:
time: 988 us; the launch traced here: 986 us
  waiting for transfers between devices  534 us (54%)
  blocking collectives  214 us (22%)
  local copies, waits for them, and re-layouts  101 us (10%)
  matrix products  77 us (8%)
  other arithmetic  34.8 us (4%)
  between operations  13.5 us (1%)
  starting transfers between devices  12.4 us (1%)
    reduce_scatter x1, waiting for transfers between devices, body(): lax.psum_scatter(partial_rows, 'section', scatter_dimension=0, tiled=True)  206 us
    all_to_all x1, blocking collectives, body(): lax.all_to_all(send_tiles.reshape(expert_count, capacity, width), 'expert...  205 us
    all_to_all x1, waiting for transfers between devices, body(): lax.all_to_all(summed_rows, 'expert', split_axis=0, concat_axis=0, tiled=...  199 us
    all_gather x1, waiting for transfers between devices, body(): lax.all_gather(got_tiles[None], 'section', axis=0, tiled=True)  129 us
    mul x2, local copies, waits for them, and re-layouts, body(): all_tiles.reshape(section_count, expert_count, capacity, tile_count, 128)  43.3 us
    another operation x1, local copies, waits for them, and re-layouts, body(): w_down[0].reshape(hidden_local, section_count, width)  33 us
    dot_general x1, matrix products, body(): jnp.einsum('rf,fsd->srd', hidden, w_down[0].reshape(hidden_local, section...  26.9 us
    dot_general x1, matrix products, body(): jnp.einsum('srd,sdf->rf', restored, w_up[0].reshape(section_count, width,...  23.7 us
  transfers between devices with their start and end apart: 4, of which 3 were waited for; matrix products, arithmetic and copies ran while one was open for 8% of the time, Pallas kernels for 0%

commit v1 on v0

--- a/solution.py
+++ b/solution.py
@@ -1,3 +1,4 @@
+import functools
 import jax
 import jax.numpy as jnp
 from jax import lax
@@ -5,6 +6,22 @@
 
 quant_limit = 448.0
 route_scaling = 2.5
+
+
+def groups_read(mat, chip_axis):
+    right_arr = jnp.concatenate(
+        lax.all_to_all(
+            jnp.stack(lax.axis_size(chip_axis) * [mat], 0),
+            axis_name=chip_axis,
+            split_axis=0,
+            concat_axis=0,
+        ),
+        0,
+    )
+    return right_arr
+
+
+see_islands_by_axis = functools.partial(groups_read, chip_axis="section")
 
 
 def slot_positions(ids, capacity, experts):
@@ -53,7 +70,7 @@
         ),
     )
     all_tiles, all_scales = (
-        lax.all_gather(got_tiles[None], "section", axis=0, tiled=True),
+        see_islands_by_axis(got_tiles[None]),
         lax.all_gather(got_scales[None], "section", axis=0, tiled=True),
     )
     restored = (

time: 988 us -> 1050 us (1.063)
  waiting for transfers between devices: 534 us -> 603 us
  blocking collectives: 214 us -> 169 us
  starting transfers between devices: 12.4 us -> 28.4 us
  other arithmetic: 34.8 us -> 50.4 us
    all_to_all x1 -> x0, blocking collectives: 205 us -> none  [body(): lax.all_to_all(send_tiles.reshape(expert_count, capacity, width), 'expert...]
    all_to_all x0 -> x2, waiting for transfers between devices: none -> 198 us  [the longest x1 198 us: body(): lax.all_to_all(send_tiles.reshape(expert_count, capacity, width), 'expert...]
    all_gather x1, blocking collectives: 8.46 us -> 169 us  [body(): lax.all_gather(got_scales[None], 'section', axis=0, tiled=True)]
    all_gather x1 -> x0, waiting for transfers between devices: 129 us -> none  [body(): lax.all_gather(got_tiles[None], 'section', axis=0, tiled=True)]
    all_to_all x0 -> x2, starting transfers between devices: none -> 17 us  [the longest x1 10.3 us: groups_read(): lax.all_to_all(jnp.stack(lax.axis_size(chip_axis) * [mat], 0), axis_name=...]
    another operation x3 -> x4, other arithmetic: 4.64 us -> 20.3 us  [the longest x1 15.7 us: groups_read(): jnp.stack(lax.axis_size(chip_axis) * [mat], 0)]
  transfers between devices with their start and end apart: 4 -> 5, of which waited for: 3 -> 3; matrix products, arithmetic and copies ran while one was open for 8% -> 9% of each run, Pallas kernels for 0% -> 0%
where the time goes in v1:
time: 1050 us; the launch traced here: 1040 us
  waiting for transfers between devices  603 us (57%)
  blocking collectives  169 us (16%)
  local copies, waits for them, and re-layouts  99.4 us (9%)
  matrix products  80.6 us (8%)
  other arithmetic  50.4 us (5%)
  starting transfers between devices  28.4 us (3%)
  between operations  13.5 us (1%)
    reduce_scatter x1, waiting for transfers between devices, body(): lax.psum_scatter(partial_rows, 'section', scatter_dimension=0, tiled=True)  207 us
    all_to_all x1, waiting for transfers between devices, body(): lax.all_to_all(summed_rows, 'expert', split_axis=0, concat_axis=0, tiled=...  199 us
    all_to_all x1, waiting for transfers between devices, body(): lax.all_to_all(send_tiles.reshape(expert_count, capacity, width), 'expert...  198 us
    all_gather x1, blocking collectives, body(): lax.all_gather(got_scales[None], 'section', axis=0, tiled=True)  169 us
    mul x2, local copies, waits for them, and re-layouts, body(): all_tiles.reshape(section_count, expert_count, capacity, tile_count, 128)  43.5 us
    another operation x1, local copies, waits for them, and re-layouts, body(): w_down[0].reshape(hidden_local, section_count, width)  32 us
    dot_general x1, matrix products, body(): jnp.einsum('rf,fsd->srd', hidden, w_down[0].reshape(hidden_local, section...  26.9 us
    dot_general x1, matrix products, body(): jnp.einsum('srd,sdf->rf', restored, w_up[0].reshape(section_count, width,...  23.7 us
  transfers between devices with their start and end apart: 5, of which 3 were waited for; matrix products, arithmetic and copies ran while one was open for 9% of the time, Pallas kernels for 0%

profile of v1, /device:TPU:11, one launch (start us, length us, event | category | flops | bytes accessed | tf_op | source)
XLA Modules:
  0.0 1044.7 jit_solution(2486354130776963056)
XLA Ops:
  6.5 0.8 copy.61
  7.3 0.1 eq.42
  7.4 0.1 eq.38
  7.5 4.5 reduce-window.6
  12.0 0.1 slice.10
  12.1 0.1 copy.63
  12.3 0.1 copy.64
  12.4 0.1 broadcast_add_fusion
  12.5 0.1 reduce_sum.30
  12.6 1.2 compare_and_fusion
  13.8 0.0 copy-start
  13.8 0.1 copy.67
  13.9 0.5 copy-done
  14.4 1.6 fusion.6
  16.1 1.6 copy.68
  17.6 0.7 multiply_exponential_fusion
  18.4 0.2 fusion.9
  18.6 6.1 convolution_convert_fusion.1
  24.8 0.0 copy-start.3
  24.8 6.7 all-to-all-start
  31.4 0.0 copy-done.3
  31.4 0.3 convolution_convert_fusion.2
  31.7 0.2 reshape.55
  31.9 0.7 copy.69
  32.6 198.0 %all-to-all-done = bf16[16,80,3584]{2,1,0:T(8,128)(2,1)} async-done(((bf16[16,80,3584]{2,1,0:T(8,128)(2,1)}), bf16[16,80,3584]{2,1,0:T(8,128)(2,1)}, u32[]{:S(2)}, u32[]{:S(2)}) %all-to-all-start) | async-done | bytes 9175072 | tf_op jit(solution)/shard_map/all_to_all | solution.py:57
  230.6 4.8 all-to-all-start.2
  235.4 15.7 %pad_maximum_fusion = bf16[2,1,16,80,3584]{4,3,2,1,0:T(8,128)(2,1)} fusion(bf16[1,1,16,80,3584]{4,3,2,1,0:T(8,128)(2,1)} %bitcast.4), kind=kLoop, calls=%fused_computation.2 | loop fusion | flops 9175040 | bytes 27525120 | tf_op jit(solution)/shard_map/stack | solution.py:14
  251.1 0.0 all-to-all-done.2
  251.1 10.3 all-to-all-start.1
  261.4 0.0 reduce-scatter.2.cloned.1.call-start
  261.4 32.0 %reshape_squeeze.11 = bf16[1024,2,3584]{2,1,0:T(2,128)(2,1)} reshape(bf16[1,1024,7168]{2,1,0:T(8,128)(2,1)} %param.13) | data formatting | bytes 29360128 | tf_op jit(solution)/shard_map/reshape;squeeze | solution.py:97
  293.5 169.0 %all-gather = bf16[32,80,28]{1,0,2:T(8,128)(2,1)S(1)} all-gather(bf16[16,80,28]{1,0,2:T(8,128)(2,1)S(1)} %copy.70), channel_id=2, replica_groups=mesh['section'=2,'expert'=16] {'section'}, dimensions={0}, use_global_device_ids=true | all-gather | bytes 215040 | tf_op jit(solution)/shard_map/all_gather | solution.py:74
  462.5 0.4 copy.71
  463.0 13.8 %mul.47 = bf16[2,16,80,28,128]{4,3,2,1,0:T(8,128)(2,1)} broadcast(bf16[2,16,80,28]{3,2,1,0:T(8,128)(2,1)S(1)} %copy.71), dimensions={0,1,2,3} | broadcast | bytes 18493440 | tf_op jit(solution)/shard_map/mul | solution.py:77
  476.8 29.7 %mul.48 = bf16[2,1280,3584]{2,1,0:T(8,128)(2,1)} reshape(bf16[2,16,80,28,128]{4,3,2,1,0:T(8,128)(2,1)} %mul.47) | data formatting | bytes 36700160 | tf_op jit(solution)/shard_map/mul | solution.py:77
  506.4 0.0 all-to-all-done.1
  506.5 12.9 %bitcast_multiply_fusion = bf16[2,1280,3584]{2,1,0:T(8,128)(2,1)S(1)} fusion(bf16[2,1280,3584]{2,1,0:T(8,128)(2,1)} %mul.48, bf16[2,1,16,80,3584]{4,3,2,1,0:T(8,128)(2,1)} %all-to-all-done.1), kind=kLoop, calls=%fused_computation.3 | loop fusion | flops 9175040 | bytes 55050240 | tf_op jit(solution)/shard_map/mul | solution.py:77
  519.4 23.7 %fusion.15 = f32[1280,1024,1]{1,0,2:T(8,128)} fusion(bf16[2,1280,3584]{2,1,0:T(8,128)(2,1)S(1)} %bitcast_multiply_fusion, bf16[2,3584,1024]{2,1,0:T(8,128)(2,1)} %bitcast.76), kind=kOutput, calls=%fused_computation.38 | convolution fusion | flops 18790481920 | bytes 38273024 | tf_op jit(solution)/shard_map/srd,sdf->rf/dot_general | solution.py:87
  543.0 23.6 %fusion.7 = bf16[1280,1024,1]{1,0,2:T(8,128)(2,1)S(1)} fusion(f32[1280,1024,1]{1,0,2:T(8,128)} %fusion.15, bf16[2,1280,3584]{2,1,0:T(8,128)(2,1)S(1)} %bitcast_multiply_fusion, bf16[2,3584,1024]{2,1,0:T(8,128)(2,1)} %bitcast.77), kind=kOutput, calls=%fused_computation.18 | convolution fusion | flops 18798346240 | bytes 40894464 | tf_op jit(solution)/shard_map/srd,sdf->rf/dot_general | solution.py:81
  566.6 26.9 %fusion = bf16[2,1280,3584]{2,1,0:T(8,128)(2,1)} fusion(bf16[1280,1024,1]{1,0,2:T(8,128)(2,1)S(1)} %fusion.7, bf16[1024,2,3584]{2,1,0:T(2,128)(2,1)} %reshape_squeeze.11), kind=kOutput, calls=%fused_computation.4 | convolution fusion | flops 18799656960 | bytes 35651584 | tf_op jit(solution)/shard_map/rf,fsd->srd/dot_general | solution.py:94
  593.5 0.0 reduce-scatter.2.cloned.1.call-update
  593.5 206.6 %reduce-scatter.2.cloned.1.call-done = bf16[1,1280,3584]{2,1,0:T(8,128)(2,1)} async-done(((bf16[2,1280,3584]{2,1,0:T(8,128)(2,1)}), bf16[1,1280,3584]{2,1,0:T(8,128)(2,1)}) %reduce-scatter.2.cloned.1.call-update) | async-done | bytes 9175056 | tf_op jit(solution)/shard_map/reduce_scatter | solution.py:100
  800.1 0.0 copy-start.1
  800.1 0.0 copy-start.4
  800.1 0.0 copy-start.2
  800.1 6.6 all-to-all-start.3
  806.8 0.0 copy-done.1
  806.8 0.1 copy.73
  806.9 0.1 reshape.60
  807.0 0.0 copy-done.4
  807.0 0.1 copy.66
  807.1 0.0 copy-done.2
  807.2 0.1 copy.74
  807.3 198.7 %all-to-all-done.3 = bf16[16,80,3584]{2,1,0:T(8,128)(2,1)} async-done(((bf16[16,80,3584]{2,1,0:T(8,128)(2,1)}), bf16[16,80,3584]{2,1,0:T(8,128)(2,1)}, u32[]{:S(2)}, u32[]{:S(2)}) %all-to-all-start.3) | async-done | bytes 9175072 | tf_op jit(solution)/shard_map/all_to_all | solution.py:104
  1006.0 18.6 %gather_fusion = bf16[1024,3584]{1,0:T(8,128)(2,1)} fusion(bf16[1280,3584]{1,0:T(8,128)(2,1)} %bitcast.14, s32[1024]{0:T(1024)S(1)} %broadcast_clamp_fusion), kind=kCustom, calls=%fused_computation | custom fusion | bytes 14684160 | tf_op jit(solution)/shard_map/jit(_take)/gather | solution.py:106
  1024.6 13.3 %multiply_reduce_fusion = bf16[128,3584]{1,0:T(8,128)(2,1)} fusion(bf16[1024,3584]{1,0:T(8,128)(2,1)} %gather_fusion, f32[128,8]{1,0:T(8,128)S(1)} %copy.74, pred[128,8]{1,0:T(8,128)(4,1)S(1)} %copy.66), kind=kLoop, calls=%fused_computation.7 | loop fusion | flops 14221312 | bytes 8262656 | tf_op jit(solution)/shard_map/reduce_sum | solution.py:108
  (10 shorter events, 0.2 us)
Async XLA Ops:
  13.8 0.6 copy-start
  24.8 6.7 copy-start.3
  24.8 205.9 %all-to-all-start = ((bf16[16,80,3584]{2,1,0:T(8,128)(2,1)}), bf16[16,80,3584]{2,1,0:T(8,128)(2,1)}, u32[]{:S(2)}, u32[]{:S(2)}) async-start(bf16[16,80,3584]{2,1,0:T(8,128)(2,1)} %bitcast.71), calls=%async_computation | async-start | bytes 18350080 | tf_op jit(solution)/shard_map/all_to_all | solution.py:57
  230.6 20.5 %all-to-all-start.2 = ((bf16[16,80,28]{1,2,0:T(8,128)(2,1)}), bf16[16,80,28]{1,2,0:T(8,128)(2,1)S(1)}, u32[]{:S(2)}, u32[]{:S(2)}) async-start(bf16[16,80,28]{1,2,0:T(8,128)(2,1)} %copy.69), calls=%async_computation.2 | async-start | bytes 262144 | tf_op jit(solution)/shard_map/all_to_all | solution.py:64
  251.1 255.4 %all-to-all-start.1 = ((bf16[2,1,16,80,3584]{4,3,2,1,0:T(8,128)(2,1)}), bf16[2,1,16,80,3584]{4,3,2,1,0:T(8,128)(2,1)}, u32[]{:S(2)}, u32[]{:S(2)}) async-start(bf16[2,1,16,80,3584]{4,3,2,1,0:T(8,128)(2,1)} %pad_maximum_fusion), calls=%async_computation.1 | async-start | bytes 36700160 | tf_op jit(solution)/shard_map/all_to_all | solution.py:13
  261.4 538.7 %reduce-scatter.2.cloned.1.call-start = ((), (), s32[]{:S(2)}) async-start(), calls=%async_computation.5 | async-start | bytes 27525120 | tf_op jit(solution)/shard_map/reduce_scatter | solution.py:100
  800.1 6.6 copy-start.1
  800.1 6.9 copy-start.4
  800.1 7.0 copy-start.2
  800.1 205.8 %all-to-all-start.3 = ((bf16[16,80,3584]{2,1,0:T(8,128)(2,1)}), bf16[16,80,3584]{2,1,0:T(8,128)(2,1)}, u32[]{:S(2)}, u32[]{:S(2)}) async-start(bf16[16,80,3584]{2,1,0:T(8,128)(2,1)} %bitcast.72), calls=%async_computation.4 | async-start | bytes 18350080 | tf_op jit(solution)/shard_map/all_to_all | solution.py:104
Sparse Core Ops, SparseCore 0:
  593.6 206.4 reduce-scatter.1
